TPU v7x, 32 devices: a whole 2x2x4 slice. The times are simulated.
32 devices in a mesh: parts: 2 (over x), ctx: 16 (over z, y, core).
Axes of the slice: x: 2, y: 2, z: 4, core: 2. Of those that a mesh axis runs over, the one named last changes fastest.
Arguments:
- query_rows: bfloat16 [2, 4096, 1536], P(None, ('parts', 'ctx')), parts along dimension 1, may hold values from -6 to 6
- key_rows: bfloat16 [2, 4096, 1536], P(None, ('parts', 'ctx')), parts along dimension 1, may hold values from -4 to 4
- value_rows: bfloat16 [2, 4096, 1536], P(None, ('parts', 'ctx')), parts along dimension 1, may hold values from -12 to 12
- step_rates: float32 [2, 4096, 4], P(None, ('parts', 'ctx')), parts along dimension 1, may hold values from 0.01 to 1
- gate_weight: float32 [3072, 384], P(('parts', 'ctx')), parts along dimension 0, may hold values from -0.3125 to 0.3125
- up_weight: float32 [3072, 384], P(('parts', 'ctx')), parts along dimension 0, may hold values from -0.3125 to 0.3125
- down_weight: float32 [3072, 384], P(('parts', 'ctx')), parts along dimension 0, may hold values from -0.3125 to 0.3125
Outputs:
- attended: bfloat16 [2, 4096, 1536], P(None, ('parts', 'ctx')), parts along dimension 1
- gate_next: float32 [3072, 384], P(('parts', 'ctx')), parts along dimension 0
- up_next: float32 [3072, 384], P(('parts', 'ctx')), parts along dimension 0
- down_next: float32 [3072, 384], P(('parts', 'ctx')), parts along dimension 0
There are 2 independent parts, one for each index of `parts`. A program takes and returns all parts, laid end to end along the dimension named above; each array names one. Nothing has to cross between parts.
All inputs are finite; a program needn't handle non-finite values.
Results may differ from a plain program's by a relative error of at most 0.0081.
Values may be sent and summed in bfloat16 or wider, within the bound.
No kernel may reach another device: no remote copies, remote signals or barrier semaphores. Data moves between devices by JAX's collectives and lax.ppermute only.
A program may use at most 64 MiB of HBM per device.

v0:
```python
import functools
import math

import jax
import jax.numpy as jnp
from jax import lax
from jax.experimental import pallas as pl
from jax.experimental.pallas import tpu as pltpu
from jax.sharding import PartitionSpec as P


SMEM = pl.BlockSpec(memory_space=pltpu.SMEM)
VMEM = pl.BlockSpec(memory_space=pltpu.VMEM)
HBM = pl.BlockSpec(memory_space=pltpu.HBM)
F32 = jnp.float32
BF16 = jnp.bfloat16


def shape_of(shape, dtype):
    return jax.ShapeDtypeStruct(shape, dtype)


def swap(value, mask):
    pairs = [(source, source ^ mask) for source in range(lax.axis_size("ctx"))]
    return lax.ppermute(value, "ctx", pairs)


def silu_parts(values):
    sig = jax.nn.sigmoid(values)
    return (values * sig, sig * (1.0 + values * (1.0 - sig)))


def mul(a, b, left, right):
    return lax.dot_general(a, b, (((left,), (right,)), ((), ())), preferred_element_type=F32)


def columns_of(head, width):
    return pl.ds(pl.multiple_of(head * width, 128), width)


def start_all(copies):
    for copy in copies:
        copy.start()
    return copies


def pack_pairs(c, ids, key_ref, value_ref, rate_ref, *refs):
    outs, (value_s, rate_s, sems) = refs[:-3], refs[-3:]
    heads, _, width = value_s.shape
    rate_copy = pltpu.make_async_copy(rate_ref.at[c], rate_s.at[pl.ds(0, heads)], sems.at[2, 0])
    rate_copy.start()
    copies = []
    for at, out in enumerate(outs):
        cols = columns_of(ids[2 + at], width)
        copies.append(start_all((
            pltpu.make_async_copy(value_ref.at[c, :, cols], value_s.at[at], sems.at[0, at]),
            pltpu.make_async_copy(key_ref.at[c, :, cols], out.at[0], sems.at[1, at]),
        )))
    rate_copy.wait()
    rates = jnp.transpose(rate_s[...])
    lanes = lax.broadcasted_iota(jnp.int32, rates.shape, 1)
    for at, out in enumerate(outs):
        rate = jnp.sum(jnp.where(lanes == ids[2 + at], rates, 0.0), axis=1, keepdims=True)
        copies[at][0].wait()
        out[1] = (rate * value_s[at].astype(F32)).astype(BF16)
        copies[at][1].wait()


def pack_own(ids, *refs):
    masters, (own, low, sems) = refs[:-3], refs[-3:]
    loads = start_all([pltpu.make_async_copy(m, own.at[at], sems.at[at]) for at, m in enumerate(masters)])
    for at, load in enumerate(loads):
        load.wait()
        low[at] = own[at].astype(BF16)


def pack_queries(ids, query_ref, *refs):
    outs, sems = refs[:-1], refs[-1]
    heads = len(outs) - 2
    width = outs[0].shape[1]
    targets = [(1, ids[2 + at], outs[at]) for at in range(heads)]
    targets += [(0, ids[2 + at], outs[heads + at // 2].at[min(at, 3 - at)]) for at in range(heads)]
    copies = start_all([
        pltpu.make_async_copy(query_ref.at[c, :, columns_of(head, width)], out, sems.at[at])
        for at, (c, head, out) in enumerate(targets)
    ])
    for copy in copies:
        copy.wait()


def gradients(keys, scaled, gate, up, down, store):
    first = mul(keys, gate, 1, 1)
    second = mul(keys, up, 1, 1)
    silu_first, slope = silu_parts(first)
    acts = (silu_first * second).astype(BF16)
    back = mul(scaled, down, 1, 0)
    d_gate = (back * second * slope).astype(BF16)
    d_up = (back * silu_first).astype(BF16)
    store(0, mul(d_gate, keys, 0, 0))
    store(1, mul(d_up, keys, 0, 0))
    store(2, mul(scaled, acts, 0, 0))


def gather_tokens(parts, key_s, scaled_s):
    count = parts[0].shape[1]
    for at, part in enumerate(parts):
        key_s[at * count : (at + 1) * count] = part[0]
        scaled_s[at * count : (at + 1) * count] = part[1]


def quarter(top, low, rows):
    return pl.ds(pl.multiple_of((2 * top + low) * rows, 16), rows)


def spread_rows(c, y, own, top, low, both, out):
    rows = own.shape[1]
    for m in range(3):
        for yy, cc, part in ((y, c, own), (1 - y, c, top), (y, 1 - c, low), (1 - y, 1 - c, both)):
            out[m, quarter(yy, cc, rows)] = part[m].astype(BF16)


def first_step(ids, *refs):
    heads = len(refs) - 9
    parts = refs[:heads]
    own, top, low, both, low_ref, full, sent, key_s, scaled_s = refs[heads:]
    c, y = ids[0], ids[1]
    spread_rows(c, y, own, top, low, both, low_ref)
    gather_tokens(parts, key_s, scaled_s)

    def store(m, grad):
        full[m] = grad
        sent[m] = grad.astype(BF16)

    gradients(key_s[...], scaled_s[...], low_ref[0], low_ref[1], low_ref[2], store)


def half_sum(ids, full, other, out):
    c = ids[0]
    rows = out.shape[2]
    for m in range(3):
        for y in range(2):
            at = quarter(y, c, rows)
            out[m, y] = (full[m, at] + other[m, at].astype(F32)).astype(BF16)


def root_mean(values, columns):
    mean = jnp.mean(values * values, axis=1, keepdims=True)
    return values * lax.rsqrt(mean + 1e-06) / math.sqrt(columns)


def second_step(ids, *refs):
    heads = len(refs) - 16
    parts = refs[:heads]
    own, top, low, both, full, other, near, far, low_ref, mine, kept, sent, total_s, key_s, scaled_s, grad_s = refs[heads:]
    c, y = ids[0], ids[1]
    rows, columns = own.shape[1:]
    for m in range(3):
        for q in range(2):
            for cc, extra in ((c, near), (1 - c, far)):
                at = quarter(q, cc, rows)
                total_s[m, at] = full[m, at] + other[m, at].astype(F32) + extra[m, q].astype(F32)
        total = jnp.sum(jnp.sum(total_s[m] * total_s[m], axis=0, keepdims=True), axis=1, keepdims=True)
        factor = lax.rsqrt(total / (4 * rows * columns) + 1e-06) / math.sqrt(columns)
        for yy, cc, master in ((y, c, own), (1 - y, c, top), (y, 1 - c, low), (1 - y, 1 - c, both)):
            at = quarter(yy, cc, rows)
            fresh = root_mean(master[m] + total_s[m, at] * factor, columns)
            low_ref[m, at] = fresh.astype(BF16)
            if master is own:
                mine[m] = fresh
    gather_tokens(parts, key_s, scaled_s)

    def store(m, grad):
        grad_s[m] = grad
        for q in range(2):
            kept[m, q] = grad_s[m, quarter(q, c, rows)]
            sent[m, q] = grad_s[m, quarter(q, 1 - c, rows)].astype(BF16)

    gradients(key_s[...], scaled_s[...], low_ref[0], low_ref[1], low_ref[2], store)


def quarter_sum(ids, kept, other, own, sent):
    y = ids[1]
    for m in range(3):
        own[m] = kept[m, y] + other[m, y].astype(F32)
        sent[m] = (kept[m, 1 - y] + other[m, 1 - y].astype(F32)).astype(BF16)


def answers(queries, low):
    gate, up, down = low
    acts = (jax.nn.silu(mul(queries, gate, 1, 1)) * mul(queries, up, 1, 1)).astype(BF16)
    return mul(acts, down, 1, 1).astype(BF16)


def answer_one(ids, *refs):
    heads = (len(refs) - 2) // 2
    parts, low, outs, query_s = refs[:heads], refs[heads], refs[heads + 1 : -1], refs[-1]
    count = parts[0].shape[0]
    for at in range(heads):
        query_s[at * count : (at + 1) * count] = parts[at][...]
    result = answers(query_s[...], [low[m] for m in range(3)])
    for at in range(heads):
        outs[at][...] = result[at * count : (at + 1) * count]


def answer_two(ids, mine, theirs, low, own, top, lower, both, kept, sent, query_s, low_s):
    c, y = ids[0], ids[1]
    count = mine.shape[1]
    spread_rows(c, y, own, top, lower, both, low_s)
    for at, weights in enumerate((low, low_s)):
        query_s[:count] = mine[at]
        query_s[count:] = theirs[at]
        result = answers(query_s[...], [weights[m] for m in range(3)])
        kept[at] = result[:count]
        sent[at] = result[count:]


def place(ids, *refs):
    parts, out, sems = refs[:-2], refs[-2], refs[-1]
    heads = len(parts) - 2
    width = parts[0].shape[1]
    sources = [(1, ids[2 + at], parts[at]) for at in range(heads)]
    sources += [(0, ids[2 + at], parts[heads + at // 2].at[min(at, 3 - at)]) for at in range(heads)]
    copies = start_all([
        pltpu.make_async_copy(part, out.at[c, :, columns_of(head, width)], sems.at[at])
        for at, (c, head, part) in enumerate(sources)
    ])
    for copy in copies:
        copy.wait()


def finish(ids, mine, share, totals, *refs):
    outs, (fresh_s, sems) = refs[:-2], refs[-2:]
    rows, columns = mine.shape[1:]
    copies = []
    for m, out in enumerate(outs):
        factor = lax.rsqrt(totals[m, 0:1, 0:1] / (4 * rows * columns) + 1e-06) / math.sqrt(columns)
        fresh_s[m] = root_mean(mine[m] + share[m] * factor, columns)
        copies += start_all([pltpu.make_async_copy(fresh_s.at[m], out, sems.at[m])])
    for copy in copies:
        copy.wait()


def call(kernel, ids, args, outs, scratch=(), far_args=False, far_outs=False, limit=16):
    given, taken = (HBM if far else VMEM for far in (far_args, far_outs))
    space = pltpu.HBM if far_args else pltpu.VMEM
    args = [pltpu.with_memory_space_constraint(a, space) for a in args]
    if not far_outs:
        outs = jax.tree.map(lambda o: pltpu.VMEM(o.shape, o.dtype), outs)
    return pl.pallas_call(
        kernel,
        out_shape=outs,
        in_specs=[SMEM] + [given] * len(args),
        out_specs=jax.tree.map(lambda _: taken, outs),
        scratch_shapes=scratch,
        compiler_params=pltpu.CompilerParams(vmem_limit_bytes=limit << 20),
    )(ids, *args)


def fast_device(query_rows, key_rows, value_rows, step_rates, gate_weight, up_weight, down_weight):
    spans, count, total_width = query_rows.shape
    heads = step_rates.shape[2]
    width = total_width // heads
    groups = lax.axis_size("ctx") // heads
    position = lax.axis_index("ctx")
    plane = position // groups
    shifts = (2, 3, 1)
    ids = jnp.stack([position & 1, position >> 1 & 1, plane] + [plane ^ s for s in shifts]).astype(jnp.int32)
    rows = gate_weight.shape[0]
    size = groups * rows
    slab = shape_of((count, width), BF16)
    two = shape_of((2, count, width), BF16)
    whole = (3, size, width)
    half = (3, 2, rows, width)
    part = (3, rows, width)
    tokens = (pltpu.VMEM((heads * count, width), BF16),) * 2

    def pair(c):
        scratch = (
            pltpu.VMEM((heads, count, width), BF16),
            pltpu.VMEM((2 * heads, count), F32),
            pltpu.SemaphoreType.DMA((3, heads)),
        )
        arrays = (key_rows, value_rows, step_rates.transpose(0, 2, 1))
        return call(functools.partial(pack_pairs, c), ids, arrays, (two,) * heads, scratch, True)

    def spread(parts):
        return [parts[0]] + [swap(parts[at + 1], s * groups) for at, s in enumerate(shifts)]

    pairs = [spread(pair(c)) for c in range(spans)]
    own, own_low = call(
        pack_own, ids, (gate_weight, up_weight, down_weight), (shape_of(part, F32), shape_of(part, BF16)),
        (pltpu.SemaphoreType.DMA((3,)),), True,
    )
    top = swap(own, 2)
    low = swap(own, 1)
    both = swap(top, 1)
    far_own = swap(own_low, 2 * groups)
    far_top = swap(far_own, 2)
    far_low = swap(far_own, 1)
    far_both = swap(far_top, 1)
    *asked, ask_mine, ask_sent = call(
        pack_queries, ids, (query_rows,), (slab,) * heads + (two,) * 2, (pltpu.SemaphoreType.DMA((2 * heads,)),), True
    )
    asked = spread(asked)
    ask_theirs = swap(ask_sent, groups)

    weights, full, sent = call(
        first_step, ids, (*pairs[0], own, top, low, both),
        (shape_of(whole, BF16), shape_of(whole, F32), shape_of(whole, BF16)), tokens,
    )
    other = swap(sent, 1)
    near = swap(call(half_sum, ids, (full, other), shape_of(half, BF16)), 2)
    far = swap(near, 1)
    told_mine, told_sent = call(
        answer_two, ids, (ask_mine, ask_theirs, weights, far_own, far_top, far_low, far_both), (two, two),
        (pltpu.VMEM((2 * count, width), BF16), pltpu.VMEM(whole, BF16)),
    )
    told_theirs = swap(told_sent, groups)
    weights, mine, kept, sent = call(
        second_step, ids, (*pairs[1], own, top, low, both, full, other, near, far),
        (shape_of(whole, BF16), shape_of(part, F32), shape_of(half, F32), shape_of(half, BF16)),
        (pltpu.VMEM(whole, F32),) + tokens + (pltpu.VMEM(whole, F32),),
    )
    told = spread(call(answer_one, ids, (*asked, weights), (slab,) * heads, tokens[:1]))
    other = swap(sent, 1)
    share, sent = call(quarter_sum, ids, (kept, other), (shape_of(part, F32), shape_of(part, BF16)))
    share = share + swap(sent, 2).astype(F32)
    totals = jnp.broadcast_to(jnp.sum(share * share, axis=(1, 2))[:, None, None], (3, 8, 128))
    totals = totals + swap(totals, 1)
    totals = totals + swap(totals, 2)
    final = call(
        finish, ids, (mine, share, totals), (shape_of((rows, width), F32),) * 3,
        (pltpu.VMEM(part, F32), pltpu.SemaphoreType.DMA((3,))), False, True,
    )
    attended = call(
        place, ids, (*told, told_mine, told_theirs), shape_of(query_rows.shape, BF16),
        (pltpu.SemaphoreType.DMA((2 * heads,)),), False, True,
    )
    return (attended, *final)


def plain_gradients(keys, scaled, low):
    gate, up, down = low
    first = mul(keys, gate, 1, 1)
    second = mul(keys, up, 1, 1)
    silu_first, slope = silu_parts(first)
    acts = (silu_first * second).astype(jnp.bfloat16)
    back = mul(scaled, down, 1, 0)
    d_gate = (back * second * slope).astype(jnp.bfloat16)
    d_up = (back * silu_first).astype(jnp.bfloat16)
    return jnp.stack([mul(d_gate, keys, 0, 0), mul(d_up, keys, 0, 0), mul(scaled, acts, 0, 0)])


def plain_answers(queries, low):
    gate, up, down = low
    acts = (jax.nn.silu(mul(queries, gate, 1, 1)) * mul(queries, up, 1, 1)).astype(jnp.bfloat16)
    return mul(acts, down, 1, 1).astype(jnp.bfloat16)


def pick(array, axis, index):
    return lax.dynamic_index_in_dim(array, index, axis, keepdims=False)


def refreshed(masters, grads, totals, per_head):
    columns = masters.shape[2]
    factor = lax.rsqrt(totals / (per_head * columns) + 1e-06) / math.sqrt(columns)
    stepped = masters + grads * factor[:, None, None]
    row_mean = jnp.mean(stepped * stepped, axis=2, keepdims=True)
    return stepped * lax.rsqrt(row_mean + 1e-06) / math.sqrt(columns)


def plain_device(query_rows, key_rows, value_rows, step_rates, gate_weight, up_weight, down_weight):
    spans, count, total_width = query_rows.shape
    heads = step_rates.shape[2]
    width = total_width // heads
    groups = lax.axis_size("ctx") // heads
    bits = groups.bit_length() - 1
    position = lax.axis_index("ctx")
    plane = position // groups
    side = [position >> level & 1 for level in range(bits)]
    shifts = sorted(range(1, heads), key=lambda m: -m.bit_length())

    def exchange(array):
        parts = [pick(array, array.ndim - 2, plane)]
        for shift in shifts:
            parts.append(swap(pick(array, array.ndim - 2, plane ^ shift), shift * groups))
        return parts

    keys = key_rows.reshape(spans, count, heads, width)
    queries = query_rows.reshape(spans, count, heads, width)
    values = value_rows.reshape(spans, count, heads, width).astype(jnp.float32)
    scaled = (step_rates[:, :, :, None] * values).astype(jnp.bfloat16)

    masters = jnp.stack([gate_weight, up_weight, down_weight])
    rows = masters.shape[1]
    pairs = [exchange(jnp.stack([keys[c], scaled[c]])) for c in range(spans)]
    asked = [exchange(queries[c]) for c in range(spans)]

    whole = masters[:, None]
    for level in reversed(range(bits)):
        other = swap(whole, 1 << level)
        low_first = side[level] == 0
        both = jnp.stack([jnp.where(low_first, whole, other), jnp.where(low_first, other, whole)], axis=2)
        whole = both.reshape(3, -1, rows, width)
    whole = whole.reshape(3, groups * rows, width)

    outs = []
    for c in range(spans):
        low = whole.astype(jnp.bfloat16)
        token_keys = jnp.concatenate([part[0] for part in pairs[c]])
        token_scaled = jnp.concatenate([part[1] for part in pairs[c]])
        grads = plain_gradients(token_keys, token_scaled, low)
        outs.append(plain_answers(jnp.concatenate(asked[c]), low))
        last = c == spans - 1
        share = grads.reshape((3,) + (2,) * bits + (rows, width))
        stops = range(bits) if last else range(bits - 1)
        for level in stops:
            axis = bits - level
            kept = pick(share, axis, side[level])
            sent = pick(share, axis, 1 - side[level]).astype(jnp.bfloat16)
            share = kept + swap(sent, 1 << level).astype(jnp.float32)
        if last:
            totals = jnp.sum(share * share, axis=(1, 2))
            for level in range(bits):
                totals = totals + swap(totals, 1 << level)
            own = lax.dynamic_slice_in_dim(whole, (position % groups) * rows, rows, 1)
            own = refreshed(own, share, totals, groups * rows)
        else:
            top = bits - 1
            share = share + swap(share.astype(jnp.bfloat16), 1 << top).astype(jnp.float32)
            for level in reversed(range(bits - 1)):
                axis = bits - level
                other = swap(share.astype(jnp.bfloat16), 1 << level).astype(jnp.float32)
                low_first = side[level] == 0
                share = jnp.stack([jnp.where(low_first, share, other), jnp.where(low_first, other, share)], axis=axis)
            share = share.reshape(3, groups * rows, width)
            totals = jnp.sum(share * share, axis=(1, 2))
            whole = refreshed(whole, share, totals, groups * rows)

    finished = []
    for c in range(spans):
        parts = outs[c].reshape(heads, count, width)
        result = jnp.zeros((count, heads, width), jnp.bfloat16)
        result = lax.dynamic_update_index_in_dim(result, parts[0], plane, 1)
        for at, shift in enumerate(shifts):
            back = swap(parts[at + 1], shift * groups)
            result = lax.dynamic_update_index_in_dim(result, back, plane ^ shift, 1)
        finished.append(result.reshape(count, total_width))
    return (jnp.stack(finished), own[0], own[1], own[2])


def solution(mesh):
    tokens = P(None, ("parts", "ctx"), None)
    weights = P(("parts", "ctx"), None)

    def per_device(*arrays):
        heads = arrays[3].shape[2]
        rows = arrays[4].shape[0]
        fast = heads == 4 and lax.axis_size("ctx") == 16 and rows % 16 == 0
        return (fast_device if fast else plain_device)(*arrays)

    return jax.shard_map(
        per_device,
        mesh=mesh,
        in_specs=(tokens,) * 4 + (weights,) * 3,
        out_specs=(tokens,) + (weights,) * 3,
        check_vma=False,
    )
```

profile of v0, /device:TPU:0, one launch (start us, length us, event | category | flops | bytes accessed | tf_op | source)
XLA Modules:
  0.0 130.2 jit_solution(2471535478401033528)
XLA Ops:
  0.7 1.6 %shard_map.104 = (f32[3,96,384]{2,1,0:T(8,128)S(1)}, bf16[3,96,384]{2,1,0:T(8,128)(2,1)S(1)}) custom-call(s32[6]{0:T(128)S(1)} %stack.27.ids, f32[96,384]{1,0:T(8,128)} %refs_0_.1, f32[96,384]{1,0:T(8,128)} %refs_1_.1, f32[96,384]{1,0:T(8,128)} %refs_2_.1), custom_call_target="tpu_custom_call" | custom-call | tf_op jit(solution)/shard_map/pallas_call | solution.py:249
  2.4 3.1 %collective-permute-start.6 = (f32[3,96,384]{2,1,0:T(8,128)S(1)}, f32[3,96,384]{2,1,0:T(8,128)S(1)}, u32[]{:S(2)}, u32[]{:S(2)}) collective-permute-start(f32[3,96,384]{2,1,0:T(8,128)S(1)} %get-tuple-element.46.refs_4_), channel_id=1, source_target_pairs={{0,2},{1,3},{2,0},{3,1},{4,6},{5,7},{6,4},{7,5},{8,10},{9,11},{10,... | collective-permute-start | bytes 1327112 | tf_op jit(solution)/shard_map/ppermute | solution.py:25
  5.4 10.2 %collective-permute-done.6.refs_5_ = f32[3,96,384]{2,1,0:T(8,128)S(1)} collective-permute-done((f32[3,96,384]{2,1,0:T(8,128)S(1)}, f32[3,96,384]{2,1,0:T(8,128)S(1)}, u32[]{:S(2)}, u32[]{:S(2)}) %collective-permute-start.6) | collective-permute-done | bytes 442400 | tf_op jit(solution)/shard_map/ppermute | solution.py:25
  15.6 1.9 %shard_map.105 = (bf16[2,128,384]{2,1,0:T(8,128)(2,1)S(1)}, bf16[2,128,384]{2,1,0:T(8,128)(2,1)S(1)}, bf16[2,128,384]{2,1,0:T(8,128)(2,1)S(1)}, bf16[2,128,384]{2,1,0:T(8,128)(2,1)S(1)}) custom-call(s32[6]{0:T(128)S(1)} %stack.27.ids, bf16[2,128,1536]{2,1,0:T(8,128)(2,1)} %key_ref.3, bf16[2,128,1536]{2,1,0:T(8,128)(2,1)} %value_ref.3, f32[2,4,128]{2,1,0:T(4,128)} %bitcast.7), custom_call_target="tpu_custom_call" | custom-call | tf_op jit(solution)/shard_map/pallas_call | solution.py:249
  17.6 2.9 %collective-permute-start.9 = (bf16[2,128,384]{2,1,0:T(8,128)(2,1)S(1)}, bf16[2,128,384]{2,1,0:T(8,128)(2,1)S(1)}, u32[]{:S(2)}, u32[]{:S(2)}) collective-permute-start(bf16[2,128,384]{2,1,0:T(8,128)(2,1)S(1)} %get-tuple-element.48), channel_id=1, source_target_pairs={{0,8},{1,9},{2,10},{3,11},{4,12},{5,13},{6,14},{7,15},{8,0},{9,1},... | collective-permute-start | bytes 589832 | tf_op jit(solution)/shard_map/ppermute | solution.py:25
  22.0 12.8 %collective-permute-done.9.refs_1_ = bf16[2,128,384]{2,1,0:T(8,128)(2,1)S(1)} collective-permute-done((bf16[2,128,384]{2,1,0:T(8,128)(2,1)S(1)}, bf16[2,128,384]{2,1,0:T(8,128)(2,1)S(1)}, u32[]{:S(2)}, u32[]{:S(2)}) %collective-permute-start.9) | collective-permute-done | bytes 196640 | tf_op jit(solution)/shard_map/ppermute | solution.py:25
  35.8 2.4 %shard_map.106 = (bf16[3,384,384]{2,1,0:T(8,128)(2,1)S(1)}, f32[3,384,384]{2,1,0:T(8,128)S(1)}, bf16[3,384,384]{2,1,0:T(8,128)(2,1)S(1)}) custom-call(s32[6]{0:T(128)S(1)} %stack.27.ids, bf16[2,128,384]{2,1,0:T(8,128)(2,1)S(1)} %get-tuple-element.47.refs_0_, bf16[2,128,384]{2,1,0:T(8,128)(2,1)S(1)} %collective-permute-done.9.refs_1_, ...), custom_call_target="tpu_custom_call" | custom-call | tf_op jit(solution)/shard_map/pallas_call | solution.py:249
  38.3 2.4 %collective-permute-done.12.other.refs_9_ = bf16[3,384,384]{2,1,0:T(8,128)(2,1)S(1)} collective-permute-done((bf16[3,384,384]{2,1,0:T(8,128)(2,1)S(1)}, bf16[3,384,384]{2,1,0:T(8,128)(2,1)S(1)}, u32[]{:S(2)}, u32[]{:S(2)}) %collective-permute-start.12) | collective-permute-done | bytes 884768 | tf_op jit(solution)/shard_map/ppermute | solution.py:25
  41.3 1.6 %collective-permute-start.13 = (bf16[3,2,96,384]{3,2,1,0:T(8,128)(2,1)S(1)}, bf16[3,2,96,384]{3,2,1,0:T(8,128)(2,1)S(1)}, u32[]{:S(2)}, u32[]{:S(2)}) collective-permute-start(bf16[3,2,96,384]{3,2,1,0:T(8,128)(2,1)S(1)} %shard_map.107), channel_id=1, source_target_pairs={{0,2},{1,3},{2,0},{3,1},{4,6},{5,7},{6,4},{7,5},{8,10},{9,11},{10,... | collective-permute-start | bytes 1327112 | tf_op jit(solution)/shard_map/ppermute | solution.py:25
  43.0 10.7 %collective-permute-done.13.refs_10_ = bf16[3,2,96,384]{3,2,1,0:T(8,128)(2,1)S(1)} collective-permute-done((bf16[3,2,96,384]{3,2,1,0:T(8,128)(2,1)S(1)}, bf16[3,2,96,384]{3,2,1,0:T(8,128)(2,1)S(1)}, u32[]{:S(2)}, u32[]{:S(2)}) %collective-permute-start.13) | collective-permute-done | bytes 442400 | tf_op jit(solution)/shard_map/ppermute | solution.py:25
  53.6 1.9 %shard_map.103 = (bf16[2,128,384]{2,1,0:T(8,128)(2,1)S(1)}, bf16[2,128,384]{2,1,0:T(8,128)(2,1)S(1)}, bf16[2,128,384]{2,1,0:T(8,128)(2,1)S(1)}, bf16[2,128,384]{2,1,0:T(8,128)(2,1)S(1)}) custom-call(s32[6]{0:T(128)S(1)} %stack.27.ids, bf16[2,128,1536]{2,1,0:T(8,128)(2,1)} %key_ref.3, bf16[2,128,1536]{2,1,0:T(8,128)(2,1)} %value_ref.3, f32[2,4,128]{2,1,0:T(4,128)} %bitcast.8), custom_call_target="tpu_custom_call" | custom-call | tf_op jit(solution)/shard_map/pallas_call | solution.py:249
  55.6 5.6 %collective-permute-start.3 = (bf16[2,128,384]{2,1,0:T(8,128)(2,1)S(1)}, bf16[2,128,384]{2,1,0:T(8,128)(2,1)S(1)}, u32[]{:S(2)}, u32[]{:S(2)}) collective-permute-start(bf16[2,128,384]{2,1,0:T(8,128)(2,1)S(1)} %get-tuple-element.43), channel_id=1, source_target_pairs={{0,8},{1,9},{2,10},{3,11},{4,12},{5,13},{6,14},{7,15},{8,0},{9,1},... | collective-permute-start | bytes 589832 | tf_op jit(solution)/shard_map/ppermute | solution.py:25
  61.8 13.6 %collective-permute-done.3.refs_1_ = bf16[2,128,384]{2,1,0:T(8,128)(2,1)S(1)} collective-permute-done((bf16[2,128,384]{2,1,0:T(8,128)(2,1)S(1)}, bf16[2,128,384]{2,1,0:T(8,128)(2,1)S(1)}, u32[]{:S(2)}, u32[]{:S(2)}) %collective-permute-start.3) | collective-permute-done | bytes 196640 | tf_op jit(solution)/shard_map/ppermute | solution.py:25
  76.5 3.4 %shard_map.108 = (bf16[3,384,384]{2,1,0:T(8,128)(2,1)S(1)}, f32[3,96,384]{2,1,0:T(8,128)S(1)}, f32[3,2,96,384]{3,2,1,0:T(8,128)S(1)}, bf16[3,2,96,384]{3,2,1,0:T(8,128)(2,1)S(1)}) custom-call(s32[6]{0:T(128)S(1)} %stack.27.ids, bf16[2,128,384]{2,1,0:T(8,128)(2,1)S(1)} %get-tuple-element.42.refs_0_, bf16[2,128,384]{2,1,0:T(8,128)(2,1)S(1)} %collective-permute-done.3.refs_1_, ...), custom_call_target="tpu_custom_call" | custom-call | tf_op jit(solution)/shard_map/pallas_call | solution.py:249
  80.1 2.7 %collective-permute-start.19 = (bf16[3,96,384]{2,1,0:T(8,128)(2,1)S(1)}, bf16[3,96,384]{2,1,0:T(8,128)(2,1)S(1)}, u32[]{:S(2)}, u32[]{:S(2)}) collective-permute-start(bf16[3,96,384]{2,1,0:T(8,128)(2,1)S(1)} %get-tuple-element.61), channel_id=1, source_target_pairs={{0,8},{1,9},{2,10},{3,11},{4,12},{5,13},{6,14},{7,15},{8,0},{9,1},... | collective-permute-start | bytes 663560 | tf_op jit(solution)/shard_map/ppermute | solution.py:25
  82.8 10.8 %collective-permute-done.19.own = bf16[3,96,384]{2,1,0:T(8,128)(2,1)S(1)} collective-permute-done((bf16[3,96,384]{2,1,0:T(8,128)(2,1)S(1)}, bf16[3,96,384]{2,1,0:T(8,128)(2,1)S(1)}, u32[]{:S(2)}, u32[]{:S(2)}) %collective-permute-start.19) | collective-permute-done | bytes 221216 | tf_op jit(solution)/shard_map/ppermute | solution.py:25
  93.5 1.5 %collective-permute-start.20 = (bf16[3,96,384]{2,1,0:T(8,128)(2,1)S(1)}, bf16[3,96,384]{2,1,0:T(8,128)(2,1)S(1)}, u32[]{:S(2)}, u32[]{:S(2)}) collective-permute-start(bf16[3,96,384]{2,1,0:T(8,128)(2,1)S(1)} %collective-permute-done.19.own), channel_id=1, source_target_pairs={{0,2},{1,3},{2,0},{3,1},{4,6},{5,7},{6,4},{7,5},{8,10},{9,11},{10,... | collective-permute-start | bytes 663560 | tf_op jit(solution)/shard_map/ppermute | solution.py:25
  96.3 1.8 %shard_map.102 = (bf16[128,384]{1,0:T(8,128)(2,1)S(1)}, bf16[128,384]{1,0:T(8,128)(2,1)S(1)}, bf16[128,384]{1,0:T(8,128)(2,1)S(1)}, bf16[128,384]{1,0:T(8,128)(2...) custom-call(s32[6]{0:T(128)S(1)} %stack.27.ids, bf16[2,128,1536]{2,1,0:T(8,128)(2,1)} %query_ref.1), custom_call_target="tpu_custom_call" | custom-call | tf_op jit(solution)/shard_map/pallas_call | solution.py:249
  98.5 3.4 %collective-permute-start = (bf16[128,384]{1,0:T(8,128)(2,1)S(1)}, bf16[128,384]{1,0:T(8,128)(2,1)S(1)}, u32[]{:S(2)}, u32[]{:S(2)}) collective-permute-start(bf16[128,384]{1,0:T(8,128)(2,1)S(1)} %get-tuple-element.39), channel_id=1, source_target_pairs={{0,8},{1,9},{2,10},{3,11},{4,12},{5,13},{6,14},{7,15},{8,0},{9,1},... | collective-permute-start | bytes 294920 | tf_op jit(solution)/shard_map/ppermute | solution.py:25
  102.6 3.8 %collective-permute-done.18.theirs = bf16[2,128,384]{2,1,0:T(8,128)(2,1)S(1)} collective-permute-done((bf16[2,128,384]{2,1,0:T(8,128)(2,1)S(1)}, bf16[2,128,384]{2,1,0:T(8,128)(2,1)S(1)}, u32[]{:S(2)}, u32[]{:S(2)}) %collective-permute-start.18) | collective-permute-done | bytes 196640 | tf_op jit(solution)/shard_map/ppermute | solution.py:25
  108.1 1.7 %shard_map.110 = (bf16[2,128,384]{2,1,0:T(8,128)(2,1)S(1)}, bf16[2,128,384]{2,1,0:T(8,128)(2,1)S(1)}) custom-call(s32[6]{0:T(128)S(1)} %stack.27.ids, bf16[2,128,384]{2,1,0:T(8,128)(2,1)S(1)} %get-tuple-element.58.mine, bf16[2,128,384]{2,1,0:T(8,128)(2,1)S(1)} %collective-permute-done.18.theirs, bf16[3,384,384]{2,1,0:T(8,128)(2,1)S(1)} %get-tuple-element.60.low, ...), custom_call_target="tpu_custom_call" | custom-call | tf_op jit(solution)/shard_map/pallas_call | solution.py:249
  109.8 2.1 %collective-permute-start.23 = (bf16[2,128,384]{2,1,0:T(8,128)(2,1)S(1)}, bf16[2,128,384]{2,1,0:T(8,128)(2,1)S(1)}, u32[]{:S(2)}, u32[]{:S(2)}) collective-permute-start(bf16[2,128,384]{2,1,0:T(8,128)(2,1)S(1)} %get-tuple-element.63), channel_id=1, source_target_pairs={{0,4},{1,5},{2,6},{3,7},{4,0},{5,1},{6,2},{7,3},{8,12},{9,13},{10,... | collective-permute-start | bytes 589832 | tf_op jit(solution)/shard_map/ppermute | solution.py:25
  113.4 3.9 %collective-permute-start.15 = (bf16[128,384]{1,0:T(8,128)(2,1)S(1)}, bf16[128,384]{1,0:T(8,128)(2,1)S(1)}, u32[]{:S(2)}, u32[]{:S(2)}) collective-permute-start(bf16[128,384]{1,0:T(8,128)(2,1)S(1)} %get-tuple-element.55), channel_id=1, source_target_pairs={{0,8},{1,9},{2,10},{3,11},{4,12},{5,13},{6,14},{7,15},{8,0},{9,1},... | collective-permute-start | bytes 294920 | tf_op jit(solution)/shard_map/ppermute | solution.py:25
  120.9 6.3 %collective-permute-done.16.refs_2_ = bf16[128,384]{1,0:T(8,128)(2,1)S(1)} collective-permute-done((bf16[128,384]{1,0:T(8,128)(2,1)S(1)}, bf16[128,384]{1,0:T(8,128)(2,1)S(1)}, u32[]{:S(2)}, u32[]{:S(2)}) %collective-permute-start.16) | collective-permute-done | bytes 98336 | tf_op jit(solution)/shard_map/ppermute | solution.py:25
  (49 shorter events, 17.4 us)
Async XLA Ops:
  2.4 13.2 %collective-permute-start.6 = (f32[3,96,384]{2,1,0:T(8,128)S(1)}, f32[3,96,384]{2,1,0:T(8,128)S(1)}, u32[]{:S(2)}, u32[]{:S(2)}) collective-permute-start(f32[3,96,384]{2,1,0:T(8,128)S(1)} %get-tuple-element.46.refs_4_), channel_id=1, source_target_pairs={{0,2},{1,3},{2,0},{3,1},{4,6},{5,7},{6,4},{7,5},{8,10},{9,11},{10,... | collective-permute-start | bytes 1327112 | tf_op jit(solution)/shard_map/ppermute | solution.py:25
  5.4 30.4 %collective-permute-start.7 = (f32[3,96,384]{2,1,0:T(8,128)S(1)}, f32[3,96,384]{2,1,0:T(8,128)S(1)}, u32[]{:S(2)}, u32[]{:S(2)}) collective-permute-start(f32[3,96,384]{2,1,0:T(8,128)S(1)} %get-tuple-element.46.refs_4_), channel_id=1, source_target_pairs={{0,1},{1,0},{2,3},{3,2},{4,5},{5,4},{6,7},{7,6},{8,9},{9,8},{10,11... | collective-permute-start | bytes 1327112 | tf_op jit(solution)/shard_map/ppermute | solution.py:25
  15.6 20.2 %collective-permute-start.8 = (f32[3,96,384]{2,1,0:T(8,128)S(1)}, f32[3,96,384]{2,1,0:T(8,128)S(1)}, u32[]{:S(2)}, u32[]{:S(2)}) collective-permute-start(f32[3,96,384]{2,1,0:T(8,128)S(1)} %collective-permute-done.6.refs_5_), channel_id=1, source_target_pairs={{0,1},{1,0},{2,3},{3,2},{4,5},{5,4},{6,7},{7,6},{8,9},{9,8},{10,11... | collective-permute-start | bytes 1327112 | tf_op jit(solution)/shard_map/ppermute | solution.py:25
  17.6 17.2 %collective-permute-start.9 = (bf16[2,128,384]{2,1,0:T(8,128)(2,1)S(1)}, bf16[2,128,384]{2,1,0:T(8,128)(2,1)S(1)}, u32[]{:S(2)}, u32[]{:S(2)}) collective-permute-start(bf16[2,128,384]{2,1,0:T(8,128)(2,1)S(1)} %get-tuple-element.48), channel_id=1, source_target_pairs={{0,8},{1,9},{2,10},{3,11},{4,12},{5,13},{6,14},{7,15},{8,0},{9,1},... | collective-permute-start | bytes 589832 | tf_op jit(solution)/shard_map/ppermute | solution.py:25
  20.4 14.3 %collective-permute-start.10 = (bf16[2,128,384]{2,1,0:T(8,128)(2,1)S(1)}, bf16[2,128,384]{2,1,0:T(8,128)(2,1)S(1)}, u32[]{:S(2)}, u32[]{:S(2)}) collective-permute-start(bf16[2,128,384]{2,1,0:T(8,128)(2,1)S(1)} %get-tuple-element.49), channel_id=1, source_target_pairs={{0,12},{1,13},{2,14},{3,15},{4,8},{5,9},{6,10},{7,11},{8,4},{9,5},... | collective-permute-start | bytes 589832 | tf_op jit(solution)/shard_map/ppermute | solution.py:25
  21.8 14.0 %collective-permute-start.11 = (bf16[2,128,384]{2,1,0:T(8,128)(2,1)S(1)}, bf16[2,128,384]{2,1,0:T(8,128)(2,1)S(1)}, u32[]{:S(2)}, u32[]{:S(2)}) collective-permute-start(bf16[2,128,384]{2,1,0:T(8,128)(2,1)S(1)} %get-tuple-element.50), channel_id=1, source_target_pairs={{0,4},{1,5},{2,6},{3,7},{4,0},{5,1},{6,2},{7,3},{8,12},{9,13},{10,... | collective-permute-start | bytes 589832 | tf_op jit(solution)/shard_map/ppermute | solution.py:25
  41.3 12.3 %collective-permute-start.13 = (bf16[3,2,96,384]{3,2,1,0:T(8,128)(2,1)S(1)}, bf16[3,2,96,384]{3,2,1,0:T(8,128)(2,1)S(1)}, u32[]{:S(2)}, u32[]{:S(2)}) collective-permute-start(bf16[3,2,96,384]{3,2,1,0:T(8,128)(2,1)S(1)} %shard_map.107), channel_id=1, source_target_pairs={{0,2},{1,3},{2,0},{3,1},{4,6},{5,7},{6,4},{7,5},{8,10},{9,11},{10,... | collective-permute-start | bytes 1327112 | tf_op jit(solution)/shard_map/ppermute | solution.py:25
  53.6 22.9 %collective-permute-start.14 = (bf16[3,2,96,384]{3,2,1,0:T(8,128)(2,1)S(1)}, bf16[3,2,96,384]{3,2,1,0:T(8,128)(2,1)S(1)}, u32[]{:S(2)}, u32[]{:S(2)}) collective-permute-start(bf16[3,2,96,384]{3,2,1,0:T(8,128)(2,1)S(1)} %collective-permute-done.13.refs_10_), channel_id=1, source_target_pairs={{0,1},{1,0},{2,3},{3,2},{4,5},{5,4},{6,7},{7,6},{8,9},{9,8},{10,11... | collective-permute-start | bytes 1327112 | tf_op jit(solution)/shard_map/ppermute | solution.py:25
  55.6 19.8 %collective-permute-start.3 = (bf16[2,128,384]{2,1,0:T(8,128)(2,1)S(1)}, bf16[2,128,384]{2,1,0:T(8,128)(2,1)S(1)}, u32[]{:S(2)}, u32[]{:S(2)}) collective-permute-start(bf16[2,128,384]{2,1,0:T(8,128)(2,1)S(1)} %get-tuple-element.43), channel_id=1, source_target_pairs={{0,8},{1,9},{2,10},{3,11},{4,12},{5,13},{6,14},{7,15},{8,0},{9,1},... | collective-permute-start | bytes 589832 | tf_op jit(solution)/shard_map/ppermute | solution.py:25
  61.2 14.2 %collective-permute-start.4 = (bf16[2,128,384]{2,1,0:T(8,128)(2,1)S(1)}, bf16[2,128,384]{2,1,0:T(8,128)(2,1)S(1)}, u32[]{:S(2)}, u32[]{:S(2)}) collective-permute-start(bf16[2,128,384]{2,1,0:T(8,128)(2,1)S(1)} %get-tuple-element.44), channel_id=1, source_target_pairs={{0,12},{1,13},{2,14},{3,15},{4,8},{5,9},{6,10},{7,11},{8,4},{9,5},... | collective-permute-start | bytes 589832 | tf_op jit(solution)/shard_map/ppermute | solution.py:25
  61.6 14.9 %collective-permute-start.5 = (bf16[2,128,384]{2,1,0:T(8,128)(2,1)S(1)}, bf16[2,128,384]{2,1,0:T(8,128)(2,1)S(1)}, u32[]{:S(2)}, u32[]{:S(2)}) collective-permute-start(bf16[2,128,384]{2,1,0:T(8,128)(2,1)S(1)} %get-tuple-element.45), channel_id=1, source_target_pairs={{0,4},{1,5},{2,6},{3,7},{4,0},{5,1},{6,2},{7,3},{8,12},{9,13},{10,... | collective-permute-start | bytes 589832 | tf_op jit(solution)/shard_map/ppermute | solution.py:25
  80.0 15.1 %collective-permute-start.24 = (bf16[3,2,96,384]{3,2,1,0:T(8,128)(2,1)S(1)}, bf16[3,2,96,384]{3,2,1,0:T(8,128)(2,1)S(1)}, u32[]{:S(2)}, u32[]{:S(2)}) collective-permute-start(bf16[3,2,96,384]{3,2,1,0:T(8,128)(2,1)S(1)} %get-tuple-element.66), channel_id=1, source_target_pairs={{0,1},{1,0},{2,3},{3,2},{4,5},{5,4},{6,7},{7,6},{8,9},{9,8},{10,11... | collective-permute-start | bytes 1327112 | tf_op jit(solution)/shard_map/ppermute | solution.py:25
  80.1 13.5 %collective-permute-start.19 = (bf16[3,96,384]{2,1,0:T(8,128)(2,1)S(1)}, bf16[3,96,384]{2,1,0:T(8,128)(2,1)S(1)}, u32[]{:S(2)}, u32[]{:S(2)}) collective-permute-start(bf16[3,96,384]{2,1,0:T(8,128)(2,1)S(1)} %get-tuple-element.61), channel_id=1, source_target_pairs={{0,8},{1,9},{2,10},{3,11},{4,12},{5,13},{6,14},{7,15},{8,0},{9,1},... | collective-permute-start | bytes 663560 | tf_op jit(solution)/shard_map/ppermute | solution.py:25
  93.5 12.8 %collective-permute-start.20 = (bf16[3,96,384]{2,1,0:T(8,128)(2,1)S(1)}, bf16[3,96,384]{2,1,0:T(8,128)(2,1)S(1)}, u32[]{:S(2)}, u32[]{:S(2)}) collective-permute-start(bf16[3,96,384]{2,1,0:T(8,128)(2,1)S(1)} %collective-permute-done.19.own), channel_id=1, source_target_pairs={{0,2},{1,3},{2,0},{3,1},{4,6},{5,7},{6,4},{7,5},{8,10},{9,11},{10,... | collective-permute-start | bytes 663560 | tf_op jit(solution)/shard_map/ppermute | solution.py:25
  95.7 10.6 %collective-permute-start.25 = (bf16[3,96,384]{2,1,0:T(8,128)(2,1)S(1)}, bf16[3,96,384]{2,1,0:T(8,128)(2,1)S(1)}, u32[]{:S(2)}, u32[]{:S(2)}) collective-permute-start(bf16[3,96,384]{2,1,0:T(8,128)(2,1)S(1)} %get-tuple-element.68), channel_id=1, source_target_pairs={{0,2},{1,3},{2,0},{3,1},{4,6},{5,7},{6,4},{7,5},{8,10},{9,11},{10,... | collective-permute-start | bytes 663560 | tf_op jit(solution)/shard_map/ppermute | solution.py:25
  98.1 8.2 %collective-permute-start.18 = (bf16[2,128,384]{2,1,0:T(8,128)(2,1)S(1)}, bf16[2,128,384]{2,1,0:T(8,128)(2,1)S(1)}, u32[]{:S(2)}, u32[]{:S(2)}) collective-permute-start(bf16[2,128,384]{2,1,0:T(8,128)(2,1)S(1)} %get-tuple-element.59), channel_id=1, source_target_pairs={{0,4},{1,5},{2,6},{3,7},{4,0},{5,1},{6,2},{7,3},{8,12},{9,13},{10,... | collective-permute-start | bytes 589832 | tf_op jit(solution)/shard_map/ppermute | solution.py:25
  98.5 13.4 %collective-permute-start = (bf16[128,384]{1,0:T(8,128)(2,1)S(1)}, bf16[128,384]{1,0:T(8,128)(2,1)S(1)}, u32[]{:S(2)}, u32[]{:S(2)}) collective-permute-start(bf16[128,384]{1,0:T(8,128)(2,1)S(1)} %get-tuple-element.39), channel_id=1, source_target_pairs={{0,8},{1,9},{2,10},{3,11},{4,12},{5,13},{6,14},{7,15},{8,0},{9,1},... | collective-permute-start | bytes 294920 | tf_op jit(solution)/shard_map/ppermute | solution.py:25
  101.9 10.0 %collective-permute-start.1 = (bf16[128,384]{1,0:T(8,128)(2,1)S(1)}, bf16[128,384]{1,0:T(8,128)(2,1)S(1)}, u32[]{:S(2)}, u32[]{:S(2)}) collective-permute-start(bf16[128,384]{1,0:T(8,128)(2,1)S(1)} %get-tuple-element.40), channel_id=1, source_target_pairs={{0,12},{1,13},{2,14},{3,15},{4,8},{5,9},{6,10},{7,11},{8,4},{9,5},... | collective-permute-start | bytes 294920 | tf_op jit(solution)/shard_map/ppermute | solution.py:25
  107.9 11.4 %collective-permute-start.26 = (f32[3,8,128]{2,1,0:T(8,128)S(1)}, f32[3,8,128]{2,1,0:T(8,128)S(1)}, u32[]{:S(2)}, u32[]{:S(2)}) collective-permute-start(f32[3,8,128]{2,1,0:T(8,128)S(1)} %broadcast_in_dim.2), channel_id=1, source_target_pairs={{0,1},{1,0},{2,3},{3,2},{4,5},{5,4},{6,7},{7,6},{8,9},{9,8},{10,11... | collective-permute-start | bytes 36872 | tf_op jit(solution)/shard_map/ppermute | solution.py:25
  109.8 11.0 %collective-permute-start.23 = (bf16[2,128,384]{2,1,0:T(8,128)(2,1)S(1)}, bf16[2,128,384]{2,1,0:T(8,128)(2,1)S(1)}, u32[]{:S(2)}, u32[]{:S(2)}) collective-permute-start(bf16[2,128,384]{2,1,0:T(8,128)(2,1)S(1)} %get-tuple-element.63), channel_id=1, source_target_pairs={{0,4},{1,5},{2,6},{3,7},{4,0},{5,1},{6,2},{7,3},{8,12},{9,13},{10,... | collective-permute-start | bytes 589832 | tf_op jit(solution)/shard_map/ppermute | solution.py:25
  113.4 7.5 %collective-permute-start.15 = (bf16[128,384]{1,0:T(8,128)(2,1)S(1)}, bf16[128,384]{1,0:T(8,128)(2,1)S(1)}, u32[]{:S(2)}, u32[]{:S(2)}) collective-permute-start(bf16[128,384]{1,0:T(8,128)(2,1)S(1)} %get-tuple-element.55), channel_id=1, source_target_pairs={{0,8},{1,9},{2,10},{3,11},{4,12},{5,13},{6,14},{7,15},{8,0},{9,1},... | collective-permute-start | bytes 294920 | tf_op jit(solution)/shard_map/ppermute | solution.py:25
  117.3 9.9 %collective-permute-start.16 = (bf16[128,384]{1,0:T(8,128)(2,1)S(1)}, bf16[128,384]{1,0:T(8,128)(2,1)S(1)}, u32[]{:S(2)}, u32[]{:S(2)}) collective-permute-start(bf16[128,384]{1,0:T(8,128)(2,1)S(1)} %get-tuple-element.56), channel_id=1, source_target_pairs={{0,12},{1,13},{2,14},{3,15},{4,8},{5,9},{6,10},{7,11},{8,4},{9,5},... | collective-permute-start | bytes 294920 | tf_op jit(solution)/shard_map/ppermute | solution.py:25
  118.8 8.4 %collective-permute-start.17 = (bf16[128,384]{1,0:T(8,128)(2,1)S(1)}, bf16[128,384]{1,0:T(8,128)(2,1)S(1)}, u32[]{:S(2)}, u32[]{:S(2)}) collective-permute-start(bf16[128,384]{1,0:T(8,128)(2,1)S(1)} %get-tuple-element.57), channel_id=1, source_target_pairs={{0,4},{1,5},{2,6},{3,7},{4,0},{5,1},{6,2},{7,3},{8,12},{9,13},{10,... | collective-permute-start | bytes 294920 | tf_op jit(solution)/shard_map/ppermute | solution.py:25
  119.4 9.3 %collective-permute-start.27 = (f32[3,8,128]{2,1,0:T(8,128)S(1)}, f32[3,8,128]{2,1,0:T(8,128)S(1)}, u32[]{:S(2)}, u32[]{:S(2)}) collective-permute-start(f32[3,8,128]{2,1,0:T(8,128)S(1)} %broadcast_add_fusion), channel_id=1, source_target_pairs={{0,2},{1,3},{2,0},{3,1},{4,6},{5,7},{6,4},{7,5},{8,10},{9,11},{10,... | collective-permute-start | bytes 36872 | tf_op jit(solution)/shard_map/ppermute | solution.py:25
  (4 other events, 11.4 us)
where the time goes:
time: 131 us; the launch traced here: 130 us
  waiting for transfers between devices  73.5 us (56%)
  starting transfers between devices  34.9 us (27%)
  Pallas kernels  20.5 us (16%)
    ppermute x28, waiting for transfers between devices, swap(): return lax.ppermute(value, 'ctx', pairs)  73.5 us
    ppermute x28, starting transfers between devices, swap(): return lax.ppermute(value, 'ctx', pairs)  34.9 us
    pallas_call x12, Pallas kernels, call(): pl.pallas_call(kernel, out_shape=outs, in_specs=[SMEM] + [given] * len(ar...  20.5 us
  transfers between devices with their start and end apart: 28, of which 12 were waited for; matrix products, arithmetic and copies ran while one was open for 0% of the time, Pallas kernels for 8%

commit v1 on v0

--- a/solution.py
+++ b/solution.py
@@ -74,12 +74,15 @@
         low[at] = own[at].astype(BF16)
 
 
+def slab_of(arrays, at):
+    return (arrays[2].at[2], arrays[0], arrays[1], arrays[3].at[2])[at]
+
+
 def pack_queries(ids, query_ref, *refs):
     outs, sems = refs[:-1], refs[-1]
-    heads = len(outs) - 2
     width = outs[0].shape[1]
-    targets = [(1, ids[2 + at], outs[at]) for at in range(heads)]
-    targets += [(0, ids[2 + at], outs[heads + at // 2].at[min(at, 3 - at)]) for at in range(heads)]
+    targets = [(1, ids[2 + at], slab_of(outs, at)) for at in range(4)]
+    targets += [(0, ids[2 + at], outs[2 + at // 2].at[min(at, 3 - at)]) for at in range(4)]
     copies = start_all([
         pltpu.make_async_copy(query_ref.at[c, :, columns_of(head, width)], out, sems.at[at])
         for at, (c, head, out) in enumerate(targets)
@@ -148,10 +151,7 @@
     return values * lax.rsqrt(mean + 1e-06) / math.sqrt(columns)
 
 
-def second_step(ids, *refs):
-    heads = len(refs) - 16
-    parts = refs[:heads]
-    own, top, low, both, full, other, near, far, low_ref, mine, kept, sent, total_s, key_s, scaled_s, grad_s = refs[heads:]
+def renew(ids, own, top, low, both, full, other, near, far, low_ref, mine, total_s):
     c, y = ids[0], ids[1]
     rows, columns = own.shape[1:]
     for m in range(3):
@@ -167,6 +167,14 @@
             low_ref[m, at] = fresh.astype(BF16)
             if master is own:
                 mine[m] = fresh
+
+
+def second_step(ids, *refs):
+    heads = len(refs) - 6
+    parts = refs[:heads]
+    low, kept, sent, key_s, scaled_s, grad_s = refs[heads:]
+    c = ids[0]
+    rows = kept.shape[2]
     gather_tokens(parts, key_s, scaled_s)
 
     def store(m, grad):
@@ -175,7 +183,7 @@
             kept[m, q] = grad_s[m, quarter(q, c, rows)]
             sent[m, q] = grad_s[m, quarter(q, 1 - c, rows)].astype(BF16)
 
-    gradients(key_s[...], scaled_s[...], low_ref[0], low_ref[1], low_ref[2], store)
+    gradients(key_s[...], scaled_s[...], low[0], low[1], low[2], store)
 
 
 def quarter_sum(ids, kept, other, own, sent):
@@ -191,22 +199,20 @@
     return mul(acts, down, 1, 1).astype(BF16)
 
 
-def answer_one(ids, *refs):
-    heads = (len(refs) - 2) // 2
-    parts, low, outs, query_s = refs[:heads], refs[heads], refs[heads + 1 : -1], refs[-1]
-    count = parts[0].shape[0]
-    for at in range(heads):
-        query_s[at * count : (at + 1) * count] = parts[at][...]
+def answer_far(ids, first, second, low, out_first, out_second, query_s):
+    count = first.shape[0]
+    query_s[:count] = first[...]
+    query_s[count:] = second[...]
     result = answers(query_s[...], [low[m] for m in range(3)])
-    for at in range(heads):
-        outs[at][...] = result[at * count : (at + 1) * count]
-
-
-def answer_two(ids, mine, theirs, low, own, top, lower, both, kept, sent, query_s, low_s):
+    out_first[...] = result[:count]
+    out_second[...] = result[count:]
+
+
+def answer_near(ids, mine, theirs, low, own, top, lower, both, fresh, kept, sent, query_s, low_s):
     c, y = ids[0], ids[1]
     count = mine.shape[1]
     spread_rows(c, y, own, top, lower, both, low_s)
-    for at, weights in enumerate((low, low_s)):
+    for at, weights in enumerate((low, low_s, fresh)):
         query_s[:count] = mine[at]
         query_s[count:] = theirs[at]
         result = answers(query_s[...], [weights[m] for m in range(3)])
@@ -214,28 +220,22 @@
         sent[at] = result[count:]
 
 
-def place(ids, *refs):
-    parts, out, sems = refs[:-2], refs[-2], refs[-1]
-    heads = len(parts) - 2
+def close(ids, mine, share, *refs):
+    norms, parts = refs[:4], refs[4:8]
+    out, masters, (fresh_s, sems) = refs[8], refs[9:12], refs[12:]
     width = parts[0].shape[1]
-    sources = [(1, ids[2 + at], parts[at]) for at in range(heads)]
-    sources += [(0, ids[2 + at], parts[heads + at // 2].at[min(at, 3 - at)]) for at in range(heads)]
+    sources = [(1, ids[2 + at], slab_of(parts, at)) for at in range(4)]
+    sources += [(0, ids[2 + at], parts[2 + at // 2].at[min(at, 3 - at)]) for at in range(4)]
     copies = start_all([
         pltpu.make_async_copy(part, out.at[c, :, columns_of(head, width)], sems.at[at])
         for at, (c, head, part) in enumerate(sources)
     ])
-    for copy in copies:
-        copy.wait()
-
-
-def finish(ids, mine, share, totals, *refs):
-    outs, (fresh_s, sems) = refs[:-2], refs[-2:]
     rows, columns = mine.shape[1:]
-    copies = []
-    for m, out in enumerate(outs):
-        factor = lax.rsqrt(totals[m, 0:1, 0:1] / (4 * rows * columns) + 1e-06) / math.sqrt(columns)
+    for m, master in enumerate(masters):
+        total = sum(norm[m, 0:1, 0:1] for norm in norms)
+        factor = lax.rsqrt(total / (4 * rows * columns) + 1e-06) / math.sqrt(columns)
         fresh_s[m] = root_mean(mine[m] + share[m] * factor, columns)
-        copies += start_all([pltpu.make_async_copy(fresh_s.at[m], out, sems.at[m])])
+        copies += start_all([pltpu.make_async_copy(fresh_s.at[m], master, sems.at[8 + m])])
     for copy in copies:
         copy.wait()
 
@@ -298,45 +298,46 @@
     far_top = swap(far_own, 2)
     far_low = swap(far_own, 1)
     far_both = swap(far_top, 1)
+    three = shape_of((3, count, width), BF16)
     *asked, ask_mine, ask_sent = call(
-        pack_queries, ids, (query_rows,), (slab,) * heads + (two,) * 2, (pltpu.SemaphoreType.DMA((2 * heads,)),), True
-    )
-    asked = spread(asked)
+        pack_queries, ids, (query_rows,), (slab,) * 2 + (three,) * 2, (pltpu.SemaphoreType.DMA((8,)),), True
+    )
+    asked = [swap(slabs, s * groups) for slabs, s in zip(asked, shifts)]
     ask_theirs = swap(ask_sent, groups)
 
-    weights, full, sent = call(
+    first_weights, full, sent = call(
         first_step, ids, (*pairs[0], own, top, low, both),
         (shape_of(whole, BF16), shape_of(whole, F32), shape_of(whole, BF16)), tokens,
     )
     other = swap(sent, 1)
     near = swap(call(half_sum, ids, (full, other), shape_of(half, BF16)), 2)
     far = swap(near, 1)
+    weights, mine = call(
+        renew, ids, (own, top, low, both, full, other, near, far),
+        (shape_of(whole, BF16), shape_of(part, F32)), (pltpu.VMEM(whole, F32),),
+    )
+    kept, sent = call(
+        second_step, ids, (*pairs[1], weights), (shape_of(half, F32), shape_of(half, BF16)),
+        tokens + (pltpu.VMEM(whole, F32),),
+    )
+    pair_s = (pltpu.VMEM((2 * count, width), BF16),)
     told_mine, told_sent = call(
-        answer_two, ids, (ask_mine, ask_theirs, weights, far_own, far_top, far_low, far_both), (two, two),
-        (pltpu.VMEM((2 * count, width), BF16), pltpu.VMEM(whole, BF16)),
-    )
-    told_theirs = swap(told_sent, groups)
-    weights, mine, kept, sent = call(
-        second_step, ids, (*pairs[1], own, top, low, both, full, other, near, far),
-        (shape_of(whole, BF16), shape_of(part, F32), shape_of(half, F32), shape_of(half, BF16)),
-        (pltpu.VMEM(whole, F32),) + tokens + (pltpu.VMEM(whole, F32),),
-    )
-    told = spread(call(answer_one, ids, (*asked, weights), (slab,) * heads, tokens[:1]))
+        answer_near, ids, (ask_mine, ask_theirs, first_weights, far_own, far_top, far_low, far_both, weights),
+        (three, three), pair_s + (pltpu.VMEM(whole, BF16),),
+    )
+    told = call(answer_far, ids, (*asked, weights), (slab,) * 2, pair_s)
+    told = [swap(slabs, s * groups) for slabs, s in zip(told, shifts)]
+    told += [told_mine, swap(told_sent, groups)]
     other = swap(sent, 1)
     share, sent = call(quarter_sum, ids, (kept, other), (shape_of(part, F32), shape_of(part, BF16)))
     share = share + swap(sent, 2).astype(F32)
-    totals = jnp.broadcast_to(jnp.sum(share * share, axis=(1, 2))[:, None, None], (3, 8, 128))
-    totals = totals + swap(totals, 1)
-    totals = totals + swap(totals, 2)
-    final = call(
-        finish, ids, (mine, share, totals), (shape_of((rows, width), F32),) * 3,
-        (pltpu.VMEM(part, F32), pltpu.SemaphoreType.DMA((3,))), False, True,
-    )
-    attended = call(
-        place, ids, (*told, told_mine, told_theirs), shape_of(query_rows.shape, BF16),
-        (pltpu.SemaphoreType.DMA((2 * heads,)),), False, True,
-    )
-    return (attended, *final)
+    norm = jnp.broadcast_to(jnp.sum(share * share, axis=(1, 2))[:, None, None], (3, 8, 128))
+    norms = [norm, swap(norm, 2), swap(norm, 3), swap(norm, 1)]
+    return call(
+        close, ids, (mine, share, *norms, *told),
+        (shape_of(query_rows.shape, BF16),) + (shape_of((rows, width), F32),) * 3,
+        (pltpu.VMEM(part, F32), pltpu.SemaphoreType.DMA((11,))), False, True,
+    )
 
 
 def plain_gradients(keys, scaled, low):

time: 131 us -> 122 us (0.931)
  starting transfers between devices: 34.9 us -> 30.7 us
  waiting for transfers between devices: 73.5 us -> 69.4 us
    ppermute x28 -> x27, starting transfers between devices: 34.9 us -> 30.7 us  [swap(): return lax.ppermute(value, 'ctx', pairs)]
    ppermute x28 -> x27, waiting for transfers between devices: 73.5 us -> 69.4 us  [swap(): return lax.ppermute(value, 'ctx', pairs)]
  transfers between devices with their start and end apart: 28 -> 27, of which waited for: 12 -> 13; matrix products, arithmetic and copies ran while one was open for 0% -> 0% of each run, Pallas kernels for 8% -> 11%
where the time goes in v1:
time: 122 us; the launch traced here: 121 us
  waiting for transfers between devices  69.4 us (57%)
  starting transfers between devices  30.7 us (25%)
  Pallas kernels  20.1 us (16%)
    ppermute x27, waiting for transfers between devices, swap(): return lax.ppermute(value, 'ctx', pairs)  69.4 us
    ppermute x27, starting transfers between devices, swap(): return lax.ppermute(value, 'ctx', pairs)  30.7 us
    pallas_call x12, Pallas kernels, call(): pl.pallas_call(kernel, out_shape=outs, in_specs=[SMEM] + [given] * len(ar...  20.1 us
  transfers between devices with their start and end apart: 27, of which 13 were waited for; matrix products, arithmetic and copies ran while one was open for 0% of the time, Pallas kernels for 11%

profile of v1, /device:TPU:0, one launch (start us, length us, event | category | flops | bytes accessed | tf_op | source)
XLA Modules:
  0.0 121.3 jit_solution(7571992839279015182)
XLA Ops:
  2.4 3.1 %collective-permute-start = (f32[3,96,384]{2,1,0:T(8,128)S(1)}, f32[3,96,384]{2,1,0:T(8,128)S(1)}, u32[]{:S(2)}, u32[]{:S(2)}) collective-permute-start(f32[3,96,384]{2,1,0:T(8,128)S(1)} %get-tuple-element.31.refs_4_.own), channel_id=1, source_target_pairs={{0,2},{1,3},{2,0},{3,1},{4,6},{5,7},{6,4},{7,5},{8,10},{9,11},{10,... | collective-permute-start | bytes 1327112 | tf_op jit(solution)/shard_map/ppermute | solution.py:25
  5.4 10.2 %collective-permute-done.refs_5_.top = f32[3,96,384]{2,1,0:T(8,128)S(1)} collective-permute-done((f32[3,96,384]{2,1,0:T(8,128)S(1)}, f32[3,96,384]{2,1,0:T(8,128)S(1)}, u32[]{:S(2)}, u32[]{:S(2)}) %collective-permute-start) | collective-permute-done | bytes 442400 | tf_op jit(solution)/shard_map/ppermute | solution.py:25
  15.6 1.9 %shard_map.103 = (bf16[2,128,384]{2,1,0:T(8,128)(2,1)S(1)}, bf16[2,128,384]{2,1,0:T(8,128)(2,1)S(1)}, bf16[2,128,384]{2,1,0:T(8,128)(2,1)S(1)}, bf16[2,128,384]{2,1,0:T(8,128)(2,1)S(1)}) custom-call(s32[6]{0:T(128)S(1)} %stack.27.ids, bf16[2,128,1536]{2,1,0:T(8,128)(2,1)} %key_ref.3, bf16[2,128,1536]{2,1,0:T(8,128)(2,1)} %value_ref.3, f32[2,4,128]{2,1,0:T(4,128)} %bitcast.7), custom_call_target="tpu_custom_call" | custom-call | tf_op jit(solution)/shard_map/pallas_call | solution.py:249
  17.6 2.9 %collective-permute-start.3 = (bf16[2,128,384]{2,1,0:T(8,128)(2,1)S(1)}, bf16[2,128,384]{2,1,0:T(8,128)(2,1)S(1)}, u32[]{:S(2)}, u32[]{:S(2)}) collective-permute-start(bf16[2,128,384]{2,1,0:T(8,128)(2,1)S(1)} %get-tuple-element.33), channel_id=1, source_target_pairs={{0,8},{1,9},{2,10},{3,11},{4,12},{5,13},{6,14},{7,15},{8,0},{9,1},... | collective-permute-start | bytes 589832 | tf_op jit(solution)/shard_map/ppermute | solution.py:25
  22.0 12.8 %collective-permute-done.3.refs_1_ = bf16[2,128,384]{2,1,0:T(8,128)(2,1)S(1)} collective-permute-done((bf16[2,128,384]{2,1,0:T(8,128)(2,1)S(1)}, bf16[2,128,384]{2,1,0:T(8,128)(2,1)S(1)}, u32[]{:S(2)}, u32[]{:S(2)}) %collective-permute-start.3) | collective-permute-done | bytes 196640 | tf_op jit(solution)/shard_map/ppermute | solution.py:25
  35.8 2.4 %shard_map.104 = (bf16[3,384,384]{2,1,0:T(8,128)(2,1)S(1)}, f32[3,384,384]{2,1,0:T(8,128)S(1)}, bf16[3,384,384]{2,1,0:T(8,128)(2,1)S(1)}) custom-call(s32[6]{0:T(128)S(1)} %stack.27.ids, bf16[2,128,384]{2,1,0:T(8,128)(2,1)S(1)} %get-tuple-element.32.refs_0_, bf16[2,128,384]{2,1,0:T(8,128)(2,1)S(1)} %collective-permute-done.3.refs_1_, ...), custom_call_target="tpu_custom_call" | custom-call | tf_op jit(solution)/shard_map/pallas_call | solution.py:249
  38.3 2.4 %collective-permute-done.6.other = bf16[3,384,384]{2,1,0:T(8,128)(2,1)S(1)} collective-permute-done((bf16[3,384,384]{2,1,0:T(8,128)(2,1)S(1)}, bf16[3,384,384]{2,1,0:T(8,128)(2,1)S(1)}, u32[]{:S(2)}, u32[]{:S(2)}) %collective-permute-start.6) | collective-permute-done | bytes 884768 | tf_op jit(solution)/shard_map/ppermute | solution.py:25
  43.0 10.7 %collective-permute-done.7.near = bf16[3,2,96,384]{3,2,1,0:T(8,128)(2,1)S(1)} collective-permute-done((bf16[3,2,96,384]{3,2,1,0:T(8,128)(2,1)S(1)}, bf16[3,2,96,384]{3,2,1,0:T(8,128)(2,1)S(1)}, u32[]{:S(2)}, u32[]{:S(2)}) %collective-permute-start.7) | collective-permute-done | bytes 442400 | tf_op jit(solution)/shard_map/ppermute | solution.py:25
  53.6 1.9 %shard_map.107 = (bf16[2,128,384]{2,1,0:T(8,128)(2,1)S(1)}, bf16[2,128,384]{2,1,0:T(8,128)(2,1)S(1)}, bf16[2,128,384]{2,1,0:T(8,128)(2,1)S(1)}, bf16[2,128,384]{2,1,0:T(8,128)(2,1)S(1)}) custom-call(s32[6]{0:T(128)S(1)} %stack.27.ids, bf16[2,128,1536]{2,1,0:T(8,128)(2,1)} %key_ref.3, bf16[2,128,1536]{2,1,0:T(8,128)(2,1)} %value_ref.3, f32[2,4,128]{2,1,0:T(4,128)} %bitcast.8), custom_call_target="tpu_custom_call" | custom-call | tf_op jit(solution)/shard_map/pallas_call | solution.py:249
  55.6 3.6 %collective-permute-start.10 = (bf16[2,128,384]{2,1,0:T(8,128)(2,1)S(1)}, bf16[2,128,384]{2,1,0:T(8,128)(2,1)S(1)}, u32[]{:S(2)}, u32[]{:S(2)}) collective-permute-start(bf16[2,128,384]{2,1,0:T(8,128)(2,1)S(1)} %get-tuple-element.41), channel_id=1, source_target_pairs={{0,12},{1,13},{2,14},{3,15},{4,8},{5,9},{6,10},{7,11},{8,4},{9,5},... | collective-permute-start | bytes 589832 | tf_op jit(solution)/shard_map/ppermute | solution.py:25
  59.2 2.6 %collective-permute-start.11 = (bf16[2,128,384]{2,1,0:T(8,128)(2,1)S(1)}, bf16[2,128,384]{2,1,0:T(8,128)(2,1)S(1)}, u32[]{:S(2)}, u32[]{:S(2)}) collective-permute-start(bf16[2,128,384]{2,1,0:T(8,128)(2,1)S(1)} %get-tuple-element.42), channel_id=1, source_target_pairs={{0,4},{1,5},{2,6},{3,7},{4,0},{5,1},{6,2},{7,3},{8,12},{9,13},{10,... | collective-permute-start | bytes 589832 | tf_op jit(solution)/shard_map/ppermute | solution.py:25
  61.7 2.9 %collective-permute-start.22 = (bf16[3,96,384]{2,1,0:T(8,128)(2,1)S(1)}, bf16[3,96,384]{2,1,0:T(8,128)(2,1)S(1)}, u32[]{:S(2)}, u32[]{:S(2)}) collective-permute-start(bf16[3,96,384]{2,1,0:T(8,128)(2,1)S(1)} %get-tuple-element.55), channel_id=1, source_target_pairs={{0,8},{1,9},{2,10},{3,11},{4,12},{5,13},{6,14},{7,15},{8,0},{9,1},... | collective-permute-start | bytes 663560 | tf_op jit(solution)/shard_map/ppermute | solution.py:25
  66.3 2.7 %collective-permute-done.11.refs_3_ = bf16[2,128,384]{2,1,0:T(8,128)(2,1)S(1)} collective-permute-done((bf16[2,128,384]{2,1,0:T(8,128)(2,1)S(1)}, bf16[2,128,384]{2,1,0:T(8,128)(2,1)S(1)}, u32[]{:S(2)}, u32[]{:S(2)}) %collective-permute-start.11) | collective-permute-done | bytes 196640 | tf_op jit(solution)/shard_map/ppermute | solution.py:25
  69.0 13.2 %collective-permute-done.9.refs_1_ = bf16[2,128,384]{2,1,0:T(8,128)(2,1)S(1)} collective-permute-done((bf16[2,128,384]{2,1,0:T(8,128)(2,1)S(1)}, bf16[2,128,384]{2,1,0:T(8,128)(2,1)S(1)}, u32[]{:S(2)}, u32[]{:S(2)}) %collective-permute-start.9) | collective-permute-done | bytes 196640 | tf_op jit(solution)/shard_map/ppermute | solution.py:25
  82.2 2.3 %shard_map.108 = (f32[3,2,96,384]{3,2,1,0:T(8,128)S(1)}, bf16[3,2,96,384]{3,2,1,0:T(8,128)(2,1)S(1)}) custom-call(s32[6]{0:T(128)S(1)} %stack.27.ids, bf16[2,128,384]{2,1,0:T(8,128)(2,1)S(1)} %get-tuple-element.39.refs_0_, bf16[2,128,384]{2,1,0:T(8,128)(2,1)S(1)} %collective-permute-done.9.refs_1_, bf16[2,128,384]{2,1,0:T(8,128)(2,1)S(1)} %collective-permute-done.10.refs_2_, ...), custom_call_target="tpu_custom_call" | custom-call | tf_op jit(solution)/shard_map/pallas_call | solution.py:249
  84.6 2.3 %collective-permute-done.22.own = bf16[3,96,384]{2,1,0:T(8,128)(2,1)S(1)} collective-permute-done((bf16[3,96,384]{2,1,0:T(8,128)(2,1)S(1)}, bf16[3,96,384]{2,1,0:T(8,128)(2,1)S(1)}, u32[]{:S(2)}, u32[]{:S(2)}) %collective-permute-start.22) | collective-permute-done | bytes 221216 | tf_op jit(solution)/shard_map/ppermute | solution.py:25
  91.0 3.3 %collective-permute-done.23.top = bf16[3,96,384]{2,1,0:T(8,128)(2,1)S(1)} collective-permute-done((bf16[3,96,384]{2,1,0:T(8,128)(2,1)S(1)}, bf16[3,96,384]{2,1,0:T(8,128)(2,1)S(1)}, u32[]{:S(2)}, u32[]{:S(2)}) %collective-permute-start.23) | collective-permute-done | bytes 221216 | tf_op jit(solution)/shard_map/ppermute | solution.py:25
  96.6 2.5 %collective-permute-done.21.theirs = bf16[3,128,384]{2,1,0:T(8,128)(2,1)S(1)} collective-permute-done((bf16[3,128,384]{2,1,0:T(8,128)(2,1)S(1)}, bf16[3,128,384]{2,1,0:T(8,128)(2,1)S(1)}, u32[]{:S(2)}, u32[]{:S(2)}) %collective-permute-start.21) | collective-permute-done | bytes 294944 | tf_op jit(solution)/shard_map/ppermute | solution.py:25
  99.1 3.4 %collective-permute-start.18 = (bf16[128,384]{1,0:T(8,128)(2,1)S(1)}, bf16[128,384]{1,0:T(8,128)(2,1)S(1)}, u32[]{:S(2)}, u32[]{:S(2)}) collective-permute-start(bf16[128,384]{1,0:T(8,128)(2,1)S(1)} %get-tuple-element.49), channel_id=1, source_target_pairs={{0,12},{1,13},{2,14},{3,15},{4,8},{5,9},{6,10},{7,11},{8,4},{9,5},... | collective-permute-start | bytes 294920 | tf_op jit(solution)/shard_map/ppermute | solution.py:25
  102.5 2.2 %shard_map.112 = (bf16[3,128,384]{2,1,0:T(8,128)(2,1)S(1)}, bf16[3,128,384]{2,1,0:T(8,128)(2,1)S(1)}) custom-call(s32[6]{0:T(128)S(1)} %stack.27.ids, bf16[3,128,384]{2,1,0:T(8,128)(2,1)S(1)} %get-tuple-element.52.mine, bf16[3,128,384]{2,1,0:T(8,128)(2,1)S(1)} %collective-permute-done.21.theirs, bf16[3,384,384]{2,1,0:T(8,128)(2,1)S(1)} %get-tuple-element.54.low, ...), custom_call_target="tpu_custom_call" | custom-call | tf_op jit(solution)/shard_map/pallas_call | solution.py:249
  104.8 2.5 %collective-permute-done.17.first = bf16[128,384]{1,0:T(8,128)(2,1)S(1)} collective-permute-done((bf16[128,384]{1,0:T(8,128)(2,1)S(1)}, bf16[128,384]{1,0:T(8,128)(2,1)S(1)}, u32[]{:S(2)}, u32[]{:S(2)}) %collective-permute-start.17) | collective-permute-done | bytes 98336 | tf_op jit(solution)/shard_map/ppermute | solution.py:25
  108.6 1.9 %collective-permute-start.19 = (bf16[128,384]{1,0:T(8,128)(2,1)S(1)}, bf16[128,384]{1,0:T(8,128)(2,1)S(1)}, u32[]{:S(2)}, u32[]{:S(2)}) collective-permute-start(bf16[128,384]{1,0:T(8,128)(2,1)S(1)} %get-tuple-element.50), channel_id=1, source_target_pairs={{0,8},{1,9},{2,10},{3,11},{4,12},{5,13},{6,14},{7,15},{8,0},{9,1},... | collective-permute-start | bytes 294920 | tf_op jit(solution)/shard_map/ppermute | solution.py:25
  110.4 2.5 %collective-permute-start.20 = (bf16[128,384]{1,0:T(8,128)(2,1)S(1)}, bf16[128,384]{1,0:T(8,128)(2,1)S(1)}, u32[]{:S(2)}, u32[]{:S(2)}) collective-permute-start(bf16[128,384]{1,0:T(8,128)(2,1)S(1)} %get-tuple-element.51), channel_id=1, source_target_pairs={{0,12},{1,13},{2,14},{3,15},{4,8},{5,9},{6,10},{7,11},{8,4},{9,5},... | collective-permute-start | bytes 294920 | tf_op jit(solution)/shard_map/ppermute | solution.py:25
  113.6 4.7 %collective-permute-done.19.refs_4_ = bf16[128,384]{1,0:T(8,128)(2,1)S(1)} collective-permute-done((bf16[128,384]{1,0:T(8,128)(2,1)S(1)}, bf16[128,384]{1,0:T(8,128)(2,1)S(1)}, u32[]{:S(2)}, u32[]{:S(2)}) %collective-permute-start.19) | collective-permute-done | bytes 98336 | tf_op jit(solution)/shard_map/ppermute | solution.py:25
  (45 shorter events, 19.7 us)
Async XLA Ops:
  2.4 13.2 %collective-permute-start = (f32[3,96,384]{2,1,0:T(8,128)S(1)}, f32[3,96,384]{2,1,0:T(8,128)S(1)}, u32[]{:S(2)}, u32[]{:S(2)}) collective-permute-start(f32[3,96,384]{2,1,0:T(8,128)S(1)} %get-tuple-element.31.refs_4_.own), channel_id=1, source_target_pairs={{0,2},{1,3},{2,0},{3,1},{4,6},{5,7},{6,4},{7,5},{8,10},{9,11},{10,... | collective-permute-start | bytes 1327112 | tf_op jit(solution)/shard_map/ppermute | solution.py:25
  5.4 30.4 %collective-permute-start.1 = (f32[3,96,384]{2,1,0:T(8,128)S(1)}, f32[3,96,384]{2,1,0:T(8,128)S(1)}, u32[]{:S(2)}, u32[]{:S(2)}) collective-permute-start(f32[3,96,384]{2,1,0:T(8,128)S(1)} %get-tuple-element.31.refs_4_.own), channel_id=1, source_target_pairs={{0,1},{1,0},{2,3},{3,2},{4,5},{5,4},{6,7},{7,6},{8,9},{9,8},{10,11... | collective-permute-start | bytes 1327112 | tf_op jit(solution)/shard_map/ppermute | solution.py:25
  15.6 20.2 %collective-permute-start.2 = (f32[3,96,384]{2,1,0:T(8,128)S(1)}, f32[3,96,384]{2,1,0:T(8,128)S(1)}, u32[]{:S(2)}, u32[]{:S(2)}) collective-permute-start(f32[3,96,384]{2,1,0:T(8,128)S(1)} %collective-permute-done.refs_5_.top), channel_id=1, source_target_pairs={{0,1},{1,0},{2,3},{3,2},{4,5},{5,4},{6,7},{7,6},{8,9},{9,8},{10,11... | collective-permute-start | bytes 1327112 | tf_op jit(solution)/shard_map/ppermute | solution.py:25
  17.6 17.2 %collective-permute-start.3 = (bf16[2,128,384]{2,1,0:T(8,128)(2,1)S(1)}, bf16[2,128,384]{2,1,0:T(8,128)(2,1)S(1)}, u32[]{:S(2)}, u32[]{:S(2)}) collective-permute-start(bf16[2,128,384]{2,1,0:T(8,128)(2,1)S(1)} %get-tuple-element.33), channel_id=1, source_target_pairs={{0,8},{1,9},{2,10},{3,11},{4,12},{5,13},{6,14},{7,15},{8,0},{9,1},... | collective-permute-start | bytes 589832 | tf_op jit(solution)/shard_map/ppermute | solution.py:25
  20.4 14.3 %collective-permute-start.4 = (bf16[2,128,384]{2,1,0:T(8,128)(2,1)S(1)}, bf16[2,128,384]{2,1,0:T(8,128)(2,1)S(1)}, u32[]{:S(2)}, u32[]{:S(2)}) collective-permute-start(bf16[2,128,384]{2,1,0:T(8,128)(2,1)S(1)} %get-tuple-element.34), channel_id=1, source_target_pairs={{0,12},{1,13},{2,14},{3,15},{4,8},{5,9},{6,10},{7,11},{8,4},{9,5},... | collective-permute-start | bytes 589832 | tf_op jit(solution)/shard_map/ppermute | solution.py:25
  21.8 14.0 %collective-permute-start.5 = (bf16[2,128,384]{2,1,0:T(8,128)(2,1)S(1)}, bf16[2,128,384]{2,1,0:T(8,128)(2,1)S(1)}, u32[]{:S(2)}, u32[]{:S(2)}) collective-permute-start(bf16[2,128,384]{2,1,0:T(8,128)(2,1)S(1)} %get-tuple-element.35), channel_id=1, source_target_pairs={{0,4},{1,5},{2,6},{3,7},{4,0},{5,1},{6,2},{7,3},{8,12},{9,13},{10,... | collective-permute-start | bytes 589832 | tf_op jit(solution)/shard_map/ppermute | solution.py:25
  41.3 12.3 %collective-permute-start.7 = (bf16[3,2,96,384]{3,2,1,0:T(8,128)(2,1)S(1)}, bf16[3,2,96,384]{3,2,1,0:T(8,128)(2,1)S(1)}, u32[]{:S(2)}, u32[]{:S(2)}) collective-permute-start(bf16[3,2,96,384]{3,2,1,0:T(8,128)(2,1)S(1)} %shard_map.105), channel_id=1, source_target_pairs={{0,2},{1,3},{2,0},{3,1},{4,6},{5,7},{6,4},{7,5},{8,10},{9,11},{10,... | collective-permute-start | bytes 1327112 | tf_op jit(solution)/shard_map/ppermute | solution.py:25
  53.6 11.0 %collective-permute-start.8 = (bf16[3,2,96,384]{3,2,1,0:T(8,128)(2,1)S(1)}, bf16[3,2,96,384]{3,2,1,0:T(8,128)(2,1)S(1)}, u32[]{:S(2)}, u32[]{:S(2)}) collective-permute-start(bf16[3,2,96,384]{3,2,1,0:T(8,128)(2,1)S(1)} %collective-permute-done.7.near), channel_id=1, source_target_pairs={{0,1},{1,0},{2,3},{3,2},{4,5},{5,4},{6,7},{7,6},{8,9},{9,8},{10,11... | collective-permute-start | bytes 1327112 | tf_op jit(solution)/shard_map/ppermute | solution.py:25
  55.6 10.7 %collective-permute-start.10 = (bf16[2,128,384]{2,1,0:T(8,128)(2,1)S(1)}, bf16[2,128,384]{2,1,0:T(8,128)(2,1)S(1)}, u32[]{:S(2)}, u32[]{:S(2)}) collective-permute-start(bf16[2,128,384]{2,1,0:T(8,128)(2,1)S(1)} %get-tuple-element.41), channel_id=1, source_target_pairs={{0,12},{1,13},{2,14},{3,15},{4,8},{5,9},{6,10},{7,11},{8,4},{9,5},... | collective-permute-start | bytes 589832 | tf_op jit(solution)/shard_map/ppermute | solution.py:25
  59.2 9.8 %collective-permute-start.11 = (bf16[2,128,384]{2,1,0:T(8,128)(2,1)S(1)}, bf16[2,128,384]{2,1,0:T(8,128)(2,1)S(1)}, u32[]{:S(2)}, u32[]{:S(2)}) collective-permute-start(bf16[2,128,384]{2,1,0:T(8,128)(2,1)S(1)} %get-tuple-element.42), channel_id=1, source_target_pairs={{0,4},{1,5},{2,6},{3,7},{4,0},{5,1},{6,2},{7,3},{8,12},{9,13},{10,... | collective-permute-start | bytes 589832 | tf_op jit(solution)/shard_map/ppermute | solution.py:25
  61.7 20.4 %collective-permute-start.9 = (bf16[2,128,384]{2,1,0:T(8,128)(2,1)S(1)}, bf16[2,128,384]{2,1,0:T(8,128)(2,1)S(1)}, u32[]{:S(2)}, u32[]{:S(2)}) collective-permute-start(bf16[2,128,384]{2,1,0:T(8,128)(2,1)S(1)} %get-tuple-element.40), channel_id=1, source_target_pairs={{0,8},{1,9},{2,10},{3,11},{4,12},{5,13},{6,14},{7,15},{8,0},{9,1},... | collective-permute-start | bytes 589832 | tf_op jit(solution)/shard_map/ppermute | solution.py:25
  61.7 25.1 %collective-permute-start.22 = (bf16[3,96,384]{2,1,0:T(8,128)(2,1)S(1)}, bf16[3,96,384]{2,1,0:T(8,128)(2,1)S(1)}, u32[]{:S(2)}, u32[]{:S(2)}) collective-permute-start(bf16[3,96,384]{2,1,0:T(8,128)(2,1)S(1)} %get-tuple-element.55), channel_id=1, source_target_pairs={{0,8},{1,9},{2,10},{3,11},{4,12},{5,13},{6,14},{7,15},{8,0},{9,1},... | collective-permute-start | bytes 663560 | tf_op jit(solution)/shard_map/ppermute | solution.py:25
  84.5 9.8 %collective-permute-start.12 = (bf16[3,2,96,384]{3,2,1,0:T(8,128)(2,1)S(1)}, bf16[3,2,96,384]{3,2,1,0:T(8,128)(2,1)S(1)}, u32[]{:S(2)}, u32[]{:S(2)}) collective-permute-start(bf16[3,2,96,384]{3,2,1,0:T(8,128)(2,1)S(1)} %get-tuple-element.45), channel_id=1, source_target_pairs={{0,1},{1,0},{2,3},{3,2},{4,5},{5,4},{6,7},{7,6},{8,9},{9,8},{10,11... | collective-permute-start | bytes 1327112 | tf_op jit(solution)/shard_map/ppermute | solution.py:25
  86.9 7.4 %collective-permute-start.23 = (bf16[3,96,384]{2,1,0:T(8,128)(2,1)S(1)}, bf16[3,96,384]{2,1,0:T(8,128)(2,1)S(1)}, u32[]{:S(2)}, u32[]{:S(2)}) collective-permute-start(bf16[3,96,384]{2,1,0:T(8,128)(2,1)S(1)} %collective-permute-done.22.own), channel_id=1, source_target_pairs={{0,2},{1,3},{2,0},{3,1},{4,6},{5,7},{6,4},{7,5},{8,10},{9,11},{10,... | collective-permute-start | bytes 663560 | tf_op jit(solution)/shard_map/ppermute | solution.py:25
  90.3 8.8 %collective-permute-start.21 = (bf16[3,128,384]{2,1,0:T(8,128)(2,1)S(1)}, bf16[3,128,384]{2,1,0:T(8,128)(2,1)S(1)}, u32[]{:S(2)}, u32[]{:S(2)}) collective-permute-start(bf16[3,128,384]{2,1,0:T(8,128)(2,1)S(1)} %get-tuple-element.53), channel_id=1, source_target_pairs={{0,4},{1,5},{2,6},{3,7},{4,0},{5,1},{6,2},{7,3},{8,12},{9,13},{10,... | collective-permute-start | bytes 884744 | tf_op jit(solution)/shard_map/ppermute | solution.py:25
  91.0 11.5 %collective-permute-start.24 = (bf16[3,96,384]{2,1,0:T(8,128)(2,1)S(1)}, bf16[3,96,384]{2,1,0:T(8,128)(2,1)S(1)}, u32[]{:S(2)}, u32[]{:S(2)}) collective-permute-start(bf16[3,96,384]{2,1,0:T(8,128)(2,1)S(1)} %collective-permute-done.22.own), channel_id=1, source_target_pairs={{0,1},{1,0},{2,3},{3,2},{4,5},{5,4},{6,7},{7,6},{8,9},{9,8},{10,11... | collective-permute-start | bytes 663560 | tf_op jit(solution)/shard_map/ppermute | solution.py:25
  94.3 8.2 %collective-permute-start.25 = (bf16[3,96,384]{2,1,0:T(8,128)(2,1)S(1)}, bf16[3,96,384]{2,1,0:T(8,128)(2,1)S(1)}, u32[]{:S(2)}, u32[]{:S(2)}) collective-permute-start(bf16[3,96,384]{2,1,0:T(8,128)(2,1)S(1)} %collective-permute-done.23.top), channel_id=1, source_target_pairs={{0,1},{1,0},{2,3},{3,2},{4,5},{5,4},{6,7},{7,6},{8,9},{9,8},{10,11... | collective-permute-start | bytes 663560 | tf_op jit(solution)/shard_map/ppermute | solution.py:25
  95.0 17.9 %collective-permute-start.13 = (bf16[3,96,384]{2,1,0:T(8,128)(2,1)S(1)}, bf16[3,96,384]{2,1,0:T(8,128)(2,1)S(1)}, u32[]{:S(2)}, u32[]{:S(2)}) collective-permute-start(bf16[3,96,384]{2,1,0:T(8,128)(2,1)S(1)} %get-tuple-element.47), channel_id=1, source_target_pairs={{0,2},{1,3},{2,0},{3,1},{4,6},{5,7},{6,4},{7,5},{8,10},{9,11},{10,... | collective-permute-start | bytes 663560 | tf_op jit(solution)/shard_map/ppermute | solution.py:25
  96.6 10.8 %collective-permute-start.17 = (bf16[128,384]{1,0:T(8,128)(2,1)S(1)}, bf16[128,384]{1,0:T(8,128)(2,1)S(1)}, u32[]{:S(2)}, u32[]{:S(2)}) collective-permute-start(bf16[128,384]{1,0:T(8,128)(2,1)S(1)} %get-tuple-element.48), channel_id=1, source_target_pairs={{0,8},{1,9},{2,10},{3,11},{4,12},{5,13},{6,14},{7,15},{8,0},{9,1},... | collective-permute-start | bytes 294920 | tf_op jit(solution)/shard_map/ppermute | solution.py:25
  99.1 8.3 %collective-permute-start.18 = (bf16[128,384]{1,0:T(8,128)(2,1)S(1)}, bf16[128,384]{1,0:T(8,128)(2,1)S(1)}, u32[]{:S(2)}, u32[]{:S(2)}) collective-permute-start(bf16[128,384]{1,0:T(8,128)(2,1)S(1)} %get-tuple-element.49), channel_id=1, source_target_pairs={{0,12},{1,13},{2,14},{3,15},{4,8},{5,9},{6,10},{7,11},{8,4},{9,5},... | collective-permute-start | bytes 294920 | tf_op jit(solution)/shard_map/ppermute | solution.py:25
  104.8 13.6 %collective-permute-start.26 = (bf16[3,128,384]{2,1,0:T(8,128)(2,1)S(1)}, bf16[3,128,384]{2,1,0:T(8,128)(2,1)S(1)}, u32[]{:S(2)}, u32[]{:S(2)}) collective-permute-start(bf16[3,128,384]{2,1,0:T(8,128)(2,1)S(1)} %get-tuple-element.57), channel_id=1, source_target_pairs={{0,4},{1,5},{2,6},{3,7},{4,0},{5,1},{6,2},{7,3},{8,12},{9,13},{10,... | collective-permute-start | bytes 884744 | tf_op jit(solution)/shard_map/ppermute | solution.py:25
  108.6 9.8 %collective-permute-start.19 = (bf16[128,384]{1,0:T(8,128)(2,1)S(1)}, bf16[128,384]{1,0:T(8,128)(2,1)S(1)}, u32[]{:S(2)}, u32[]{:S(2)}) collective-permute-start(bf16[128,384]{1,0:T(8,128)(2,1)S(1)} %get-tuple-element.50), channel_id=1, source_target_pairs={{0,8},{1,9},{2,10},{3,11},{4,12},{5,13},{6,14},{7,15},{8,0},{9,1},... | collective-permute-start | bytes 294920 | tf_op jit(solution)/shard_map/ppermute | solution.py:25
  110.4 7.9 %collective-permute-start.20 = (bf16[128,384]{1,0:T(8,128)(2,1)S(1)}, bf16[128,384]{1,0:T(8,128)(2,1)S(1)}, u32[]{:S(2)}, u32[]{:S(2)}) collective-permute-start(bf16[128,384]{1,0:T(8,128)(2,1)S(1)} %get-tuple-element.51), channel_id=1, source_target_pairs={{0,12},{1,13},{2,14},{3,15},{4,8},{5,9},{6,10},{7,11},{8,4},{9,5},... | collective-permute-start | bytes 294920 | tf_op jit(solution)/shard_map/ppermute | solution.py:25
  113.2 5.2 %collective-permute-start.14 = (f32[3,8,128]{2,1,0:T(8,128)S(1)}, f32[3,8,128]{2,1,0:T(8,128)S(1)}, u32[]{:S(2)}, u32[]{:S(2)}) collective-permute-start(f32[3,8,128]{2,1,0:T(8,128)S(1)} %broadcast_in_dim.2.refs_0_), channel_id=1, source_target_pairs={{0,2},{1,3},{2,0},{3,1},{4,6},{5,7},{6,4},{7,5},{8,10},{9,11},{10,... | collective-permute-start | bytes 36872 | tf_op jit(solution)/shard_map/ppermute | solution.py:25
  (3 other events, 8.4 us)
